TPU v7x, 512 devices: a whole 4x4x16 slice. The times are simulated.
512 devices in a mesh: ctx: 128 (over x, z, core), head: 4 (over y).
Axes of the slice: x: 4, y: 4, z: 16, core: 2. Of those that a mesh axis runs over, the one named last changes fastest.
Arguments:
- queries: bfloat16 [4, 16384, 1024], P(None, 'ctx', 'head'), may hold values from -45 to 45
- keys: bfloat16 [4, 16384, 1024], P(None, 'ctx', 'head'), may hold values from -6 to 6
- values: bfloat16 [4, 16384, 1024], P(None, 'ctx', 'head'), may hold values from -6 to 6
- out_weight: bfloat16 [1024, 2048], P(None, 'head'), may hold values from -0.1875 to 0.1875
- global_ids: int32 [4, 2], replicated, may hold values from 0 to 255, as said below
- rand_ids: int32 [4, 256, 4], P(None, 'ctx'), may hold values from 0 to 255, as said below
- rand_count: int32 [4, 256], P(None, 'ctx'), may hold values from 1 to 4
Outputs:
- output: bfloat16 [4, 16384, 2048], P(None, 'ctx', 'head')
Inputs may be any that keep to these rules, and one draw needn't show every extreme that they name: `global_ids`: block ids; the 2 ids of one sequence are distinct. `rand_ids`: block ids of the same sequence. Taking together the 2 query blocks that each of the 4 sequences has on one index of ctx, at most 1 live slots name blocks held by any one index of ctx.
All inputs are finite; a program needn't handle non-finite values.
Results may differ from a plain program's by a relative error of at most 0.0056.
Values may be sent and summed in bfloat16 or wider, within the bound.
A program may use at most 64 MiB of HBM per device.

v0:
```python
import jax
import jax.numpy as jnp
from jax import lax
from jax.sharding import PartitionSpec as P

HEAD_DIM = 128
BLOCK = 64
GLOB = 2
RMAX = 4


def with_halo(cells, sides, width):
    for axis, dim in sides:
        count = lax.axis_size(axis)
        head = lax.slice_in_dim(cells, 0, width, axis=dim)
        tail = lax.slice_in_dim(cells, cells.shape[dim] - width, cells.shape[dim], axis=dim)
        cells = jnp.concatenate(
            [
                lax.ppermute(tail, axis, [(i, (i + 1) % count) for i in range(count)]),
                cells,
                lax.ppermute(head, axis, [((i + 1) % count, i) for i in range(count)]),
            ],
            axis=dim,
        )
    return cells


def slot_table(slot_of, live_flat, slot_total):
    return (
        (slot_of[:, None] == jnp.arange(slot_total, dtype=jnp.int32)[None, :]) & live_flat[:, None]
    ).astype(jnp.int32)


def on_device(queries, keys, values, out_weight, global_ids, rand_ids, rand_count):
    seq_count, seq_rows, local_width = queries.shape
    blocks_here = seq_rows // BLOCK
    heads_here = local_width // HEAD_DIM
    cycle_size = lax.axis_size("ctx")
    my_index = lax.axis_index("ctx")
    request_count = seq_count * blocks_here * RMAX
    capacity = (request_count + cycle_size - 1) // cycle_size
    slot_total = cycle_size * capacity
    key_width = 3 + GLOB + RMAX
    score_scale = HEAD_DIM ** (-0.5)
    token_pairs = jnp.stack([keys, values], 0)
    block_pairs = jnp.stack(
        [
            keys.reshape(seq_count, blocks_here, BLOCK, local_width),
            values.reshape(seq_count, blocks_here, BLOCK, local_width),
        ],
        2,
    ).reshape(seq_count * blocks_here, 2, BLOCK, local_width)
    extended = with_halo(token_pairs, (("ctx", 2),), BLOCK)
    own_blocks = token_pairs.reshape(2, seq_count, blocks_here, BLOCK, local_width)
    shared_owner = global_ids // blocks_here
    shared_local = global_ids % blocks_here
    picker = (
        (shared_local[:, :, None] == jnp.arange(blocks_here, dtype=jnp.int32)[None, None, :])
        & (shared_owner == my_index)[:, :, None]
    ).astype(jnp.bfloat16)
    contribution = jnp.einsum(
        "sgj,xsjtf->xsgtf", picker, own_blocks, preferred_element_type=jnp.float32
    )
    shared_rows = lax.psum(contribution, "ctx").astype(jnp.bfloat16)
    slot_ids = jnp.arange(RMAX, dtype=jnp.int32)
    live_flat = (slot_ids[None, None, :] < rand_count[:, :, None]).reshape(-1)
    owners = (rand_ids // blocks_here).reshape(-1)
    seq_of = jnp.arange(seq_count, dtype=jnp.int32)[:, None, None]
    block_codes = (seq_of * blocks_here + rand_ids % blocks_here).reshape(-1)
    hit_owner = (
        (owners[:, None] == jnp.arange(cycle_size, dtype=jnp.int32)[None, :]) & live_flat[:, None]
    ).astype(jnp.int32)
    rank_within = jnp.sum((jnp.cumsum(hit_owner, axis=0) - hit_owner) * hit_owner, axis=1)
    slot_of = jnp.where(live_flat, owners * capacity + rank_within, 0)
    slot_hits = slot_table(slot_of, live_flat, slot_total)
    requests_out = (jnp.sum(slot_hits * (block_codes[:, None] + 1), axis=0) - 1).reshape(
        cycle_size, capacity
    )
    wanted_here = lax.all_to_all(requests_out, "ctx", split_axis=0, concat_axis=0, tiled=True)
    beside_all = extended.reshape(2, seq_count, blocks_here + 2, BLOCK, local_width)
    window_keys = jnp.stack(
        [beside_all[:, :, offset : offset + blocks_here] for offset in range(3)], 3
    )
    shared_wide = jnp.broadcast_to(
        shared_rows[:, :, None], (2, seq_count, blocks_here, GLOB, BLOCK, local_width)
    )
    local_keys = jnp.concatenate([window_keys, shared_wide], 3)
    query_view = queries.reshape(seq_count, blocks_here, BLOCK, heads_here, HEAD_DIM)
    payload = jnp.take(block_pairs, jnp.maximum(wanted_here, 0).reshape(-1), axis=0).reshape(
        cycle_size, capacity, 2, BLOCK, local_width
    )
    received = lax.all_to_all(payload, "ctx", split_axis=0, concat_axis=0, tiled=True)
    random_rows = jnp.take(received.reshape(slot_total, 2, BLOCK, local_width), slot_of, axis=0)
    random_rows = jnp.moveaxis(
        random_rows.reshape(seq_count, blocks_here, RMAX, 2, BLOCK, local_width), 3, 0
    )
    all_keys = jnp.concatenate([local_keys, random_rows], 3).reshape(
        2, seq_count, blocks_here, key_width * BLOCK, heads_here, HEAD_DIM
    )
    scores = (
        jnp.einsum(
            "sjqhd,sjkhd->sjhqk", query_view, all_keys[0], preferred_element_type=jnp.float32
        )
        * score_scale
    )
    live_slots = jnp.concatenate(
        [
            jnp.ones((seq_count, blocks_here, 3 + GLOB), jnp.bool_),
            slot_ids[None, None, :] < rand_count[:, :, None],
        ],
        2,
    )
    live_cols = jnp.repeat(live_slots, BLOCK, axis=2)[:, :, None, None, :]
    masked = jnp.where(live_cols, scores, -1e30)
    row_peak = jnp.max(masked, axis=-1, keepdims=True)
    weights = jnp.where(live_cols, jnp.exp(masked - row_peak), 0.0)
    row_total = jnp.sum(weights, axis=-1)
    weighted = jnp.einsum(
        "sjhqk,sjkhd->sjqhd",
        weights.astype(jnp.bfloat16),
        all_keys[1],
        preferred_element_type=jnp.float32,
    )
    attention = (
        (weighted / jnp.moveaxis(row_total, 2, 3)[..., None])
        .astype(jnp.bfloat16)
        .reshape(seq_count, seq_rows, local_width)
    )
    projected = jnp.einsum(
        "stf,fo->sto",
        lax.all_gather(attention, "head", axis=2, tiled=True),
        out_weight,
        preferred_element_type=jnp.float32,
    )
    return projected.astype(jnp.bfloat16)


def solution(mesh):
    placed = (
        P(None, "ctx", "head"),
        P(None, "ctx", "head"),
        P(None, "ctx", "head"),
        P(None, "head"),
        P(),
        P(None, "ctx", None),
        P(None, "ctx"),
    )
    return jax.shard_map(
        on_device, mesh=mesh, in_specs=placed, out_specs=P(None, "ctx", "head"), check_vma=False
    )
```

profile of v0, /device:TPU:2, one launch (start us, length us, event | category | flops | bytes accessed | tf_op | source)
XLA Modules:
  0.0 992.5 jit_solution(1690685669492652247)
XLA Ops:
  6.5 0.0 copy-start
  6.5 0.9 copy.54
  7.4 0.1 iota_compare_fusion.2
  7.5 0.1 lt.84
  7.6 0.8 and_select_fusion.1
  8.3 0.1 reshape.187
  8.4 0.1 fusion.37
  8.5 0.1 reduce_window_sum.11
  8.5 0.2 select_reduce_fusion.1
  8.7 0.1 add.104
  8.8 0.1 select_reduce_fusion
  8.9 0.7 copy.55
  9.7 19.5 %all-to-all-start = ((s32[128,1,1]{2,1,0:T(1,128)}), s32[128,1,1]{2,1,0:T(1,128)S(1)}, u32[]{:S(2)}, u32[]{:S(2)}) async-start(s32[128,1,1]{2,1,0:T(1,128)} %copy.55), calls=%async_computation | async-start | bytes 131072 | tf_op jit(solution)/shard_map/all_to_all | solution.py:79
  29.2 1.1 pad_maximum_fusion.3
  30.3 13.3 %all-to-all-done = s32[128,1,1]{2,1,0:T(1,128)S(1)} async-done(((s32[128,1,1]{2,1,0:T(1,128)}), s32[128,1,1]{2,1,0:T(1,128)S(1)}, u32[]{:S(2)}, u32[]{:S(2)}) %all-to-all-start) | async-done | bytes 544 | tf_op jit(solution)/shard_map/all_to_all | solution.py:79
  43.6 2.4 maximum_reduce_fusion
  46.0 6.3 gather_fusion
  52.3 2.4 compare_reduce_fusion
  54.6 7.4 bitcast_select_fusion
  62.1 8.6 all-to-all-start.1
  70.7 0.0 all-gather.2.cloned.1.call-start
  70.7 0.0 copy-done.1
  70.8 0.0 copy-done.2
  70.8 2.1 collective-permute-start
  72.9 5.6 collective-permute-start.1
  78.5 0.1 reshape.189
  78.6 0.1 lt.87
  78.7 0.3 copy.49
  79.0 0.3 copy.50
  79.3 0.1 copy.51
  79.4 0.1 copy.52
  79.5 1.8 convolution_bitcast_fusion
  81.2 774.6 %all-reduce.2 = bf16[2,4,2,64,256]{4,2,3,0,1:T(2,128)(2,1)S(1)} all-reduce(f32[2,4,2,64,256]{4,2,3,0,1:T(2,128)} %convolution_bitcast_fusion), channel_id=1, replica_groups=mesh['ctx'=128,'head'=4] {'ctx'}, use_global_device_ids=true, to_apply=%region_0.1 | all-reduce | flops 262144 | bytes 1572864 | tf_op jit(solution)/shard_map/psum | solution.py:64
  855.8 0.1 reduce_sum.32
  855.9 0.1 copy.53
  856.0 0.0 copy-done.4
  856.0 0.8 reshape.190
  856.8 0.1 concatenate.13.clone
  856.9 0.1 broadcast_in_dim.78
  857.0 0.1 broadcast_in_dim.79
  857.1 0.1 compare_and_fusion
  857.2 0.0 collective-permute-done
  857.2 0.0 collective-permute-done.1
  857.2 1.1 pad_maximum_fusion
  858.3 0.8 fusion.32
  859.1 0.8 fusion.31
  859.9 0.8 fusion.30
  860.8 1.1 broadcast_dynamic-update-slice_fusion
  861.9 0.0 all-to-all-done.1
  861.9 4.1 gather_fusion.1
  866.0 2.3 bitcast_dynamic-update-slice_fusion
  868.3 5.2 fusion.51
  873.5 4.6 squeeze.7
  878.1 5.7 squeeze.6
  883.9 1.9 fusion.6
  885.7 0.0 copy-start.3
  885.8 1.2 fusion.52
  886.9 0.5 copy-done.3
  887.4 0.6 fusion.24
  888.0 0.3 copy.65
  888.3 0.9 reshape.191
  889.2 0.0 all-gather.2.cloned.1.call-update
  889.2 93.7 %all-gather.2.cloned.1.call-done = bf16[4,128,1024]{2,1,0:T(8,128)(2,1)} async-done(((bf16[4,128,256]{2,1,0:T(8,128)(2,1)}), bf16[4,128,1024]{2,1,0:T(8,128)(2,1)}) %all-gather.2.cloned.1.call-update) | async-done | bytes 1048592 | tf_op jit(solution)/shard_map/all_gather | solution.py:131
  982.9 2.7 convolution_convert_fusion
  (17 shorter events, 0.1 us)
Async XLA Ops:
  6.5 976.4 %copy-start = (bf16[1024,512]{1,0:T(8,128)(2,1)S(1)}, bf16[1024,512]{1,0:T(8,128)(2,1)}, u32[]{:S(2)}) copy-start(bf16[1024,512]{1,0:T(8,128)(2,1)} %param.10) | copy-start | bytes 3145732
  9.7 33.9 %all-to-all-start = ((s32[128,1,1]{2,1,0:T(1,128)}), s32[128,1,1]{2,1,0:T(1,128)S(1)}, u32[]{:S(2)}, u32[]{:S(2)}) async-start(s32[128,1,1]{2,1,0:T(1,128)} %copy.55), calls=%async_computation | async-start | bytes 131072 | tf_op jit(solution)/shard_map/all_to_all | solution.py:79
  62.0 8.7 copy-start.1
  62.0 8.7 copy-start.2
  62.1 17.2 %copy-start.5 = (s32[4,2]{0,1:T(2,128)S(1)}, s32[4,2]{0,1:T(2,128)}, u32[]{:S(2)}) copy-start(s32[4,2]{0,1:T(2,128)} %param.11) | copy-start | bytes 100
  62.1 799.9 %all-to-all-start.1 = ((bf16[128,1,2,64,256]{4,3,2,1,0:T(8,128)(2,1)}), bf16[128,1,2,64,256]{4,3,2,1,0:T(8,128)(2,1)}, u32[]{:S(2)}, u32[]{:S(2)}) async-start(bf16[128,1,2,64,256]{4,3,2,1,0:T(8,128)(2,1)} %bitcast_select_fusion), calls=%async_computation.1 | async-start | bytes 16777216 | tf_op jit(solution)/shard_map/all_to_all | solution.py:92
  70.7 912.2 %all-gather.2.cloned.1.call-start = ((), (), s32[]{:S(2)}) async-start(), calls=%async_computation.2 | async-start | bytes 1310720 | tf_op jit(solution)/shard_map/all_gather | solution.py:131
  70.8 786.3 %collective-permute-start = (bf16[2,4,64,256]{3,2,1,0:T(8,128)(2,1)S(1)}, bf16[2,4,64,256]{3,2,1,0:T(8,128)(2,1)}, u32[]{:S(2)}, u32[]{:S(2)}) collective-permute-start(bf16[2,4,64,256]{3,2,1,0:T(8,128)(2,1)S(1)} %get-tuple-element.7), channel_id=1, source_target_pairs={{0,4},{4,8},{8,12},{12,16},{16,20},{20,24},{24,28},{28,32},{32,36}... | collective-permute-start | bytes 786440 | tf_op jit(solution)/shard_map/ppermute | solution.py:19
  72.9 784.3 %collective-permute-start.1 = (bf16[2,4,64,256]{3,2,1,0:T(8,128)(2,1)S(1)}, bf16[2,4,64,256]{3,2,1,0:T(8,128)(2,1)}, u32[]{:S(2)}, u32[]{:S(2)}) collective-permute-start(bf16[2,4,64,256]{3,2,1,0:T(8,128)(2,1)S(1)} %get-tuple-element.8), channel_id=1, source_target_pairs={{4,0},{8,4},{12,8},{16,12},{20,16},{24,20},{28,24},{32,28},{36,32}... | collective-permute-start | bytes 786440 | tf_op jit(solution)/shard_map/ppermute | solution.py:21
  79.5 776.5 %copy-start.4 = (bf16[4,128,256]{2,1,0:T(8,128)(2,1)S(1)}, bf16[4,128,256]{2,1,0:T(8,128)(2,1)}, u32[]{:S(2)}) copy-start(bf16[4,128,256]{2,1,0:T(8,128)(2,1)} %param.7) | copy-start | bytes 786436
  885.7 1.7 copy-start.3
Sparse Core Ops, SparseCore 0:
  889.3 93.5 all-gather.1
where the time goes:
time: 993 us; the launch traced here: 992 us
  blocking collectives  775 us (78%)
  waiting for transfers between devices  107 us (11%)
  starting transfers between devices  35.9 us (4%)
  local copies, waits for them, and re-layouts  35.2 us (4%)
  other arithmetic  19.2 us (2%)
  between operations  13.6 us (1%)
    psum x1, blocking collectives, on_device(): shared_rows = lax.psum(contribution, 'ctx').astype(jnp.bfloat16)  775 us
    all_gather x1, waiting for transfers between devices, on_device(): lax.all_gather(attention, 'head', axis=2, tiled=True)  93.7 us
  transfers between devices with their start and end apart: 5, of which 2 were waited for; matrix products, arithmetic and copies ran while one was open for 1% of the time, Pallas kernels for 0%

commit v1 on v0

--- a/solution.py
+++ b/solution.py
@@ -7,6 +7,22 @@
 BLOCK = 64
 GLOB = 2
 RMAX = 4
+
+
+def get_bars(u, point):
+    long_array, next_value, top = (lax.psum(1, "head"), lax.axis_index("head"), u.shape[2])
+    bank = tuple(((k0, (k0 + 1) % long_array) for k0 in range(long_array)))
+    shaped = long_array // 2
+    state_now = fresh = u
+    carry = point(u, next_value * top)
+    made = tuple(((k0, (k0 - 1) % long_array) for k0 in range(long_array)))
+    for d in range(1, shaped + 1):
+        state_now = lax.ppermute(state_now, "head", bank)
+        if d < long_array - shaped:
+            fresh = lax.ppermute(fresh, "head", made)
+            carry = carry + point(fresh, (next_value + d) % long_array * top)
+        carry = carry + point(state_now, (next_value - d) % long_array * top)
+    return carry
 
 
 def with_halo(cells, sides, width):
@@ -126,11 +142,14 @@
         .astype(jnp.bfloat16)
         .reshape(seq_count, seq_rows, local_width)
     )
-    projected = jnp.einsum(
-        "stf,fo->sto",
-        lax.all_gather(attention, "head", axis=2, tiled=True),
-        out_weight,
-        preferred_element_type=jnp.float32,
+    projected = get_bars(
+        attention,
+        lambda own_block, start: jnp.einsum(
+            "stf,fo->sto",
+            own_block,
+            lax.dynamic_slice_in_dim(out_weight, start, own_block.shape[2], axis=0),
+            preferred_element_type=jnp.float32,
+        ),
     )
     return projected.astype(jnp.bfloat16)
 

time: 993 us -> 973 us (0.980)
  the two profiles are of different devices: /device:TPU:2 before, /device:TPU:16 now
where the time goes in v1:
time: 973 us
  blocking collectives  844 us (87%)
  starting transfers between devices  45.3 us (5%)
  local copies, waits for them, and re-layouts  34.5 us (4%)
  waiting for transfers between devices  22.7 us (2%)
  other arithmetic  19.2 us (2%)
    psum x1, blocking collectives, on_device(): shared_rows = lax.psum(contribution, 'ctx').astype(jnp.bfloat16)  844 us
    all_to_all x1, starting transfers between devices, on_device(): lax.all_to_all(requests_out, 'ctx', split_axis=0, concat_axis=0, tiled=True)  19.8 us
  transfers between devices with their start and end apart: 7, of which 3 were waited for; matrix products, arithmetic and copies ran while one was open for 1% of the time, Pallas kernels for 0%

profile of v1, /device:TPU:16, one launch (start us, length us, event | category | flops | bytes accessed | tf_op | source)
XLA Modules:
  0.0 972.6 jit_solution(10919166663085651145)
XLA Ops:
  0.0 0.9 copy.54
  0.9 0.1 iota_compare_fusion.2
  0.9 0.1 lt.110
  1.0 0.8 and_select_fusion.1
  1.8 0.1 reshape.187
  1.9 0.1 fusion.46
  2.0 0.1 reduce_window_sum.11
  2.0 0.2 select_reduce_fusion.1
  2.2 0.1 add.140
  2.3 0.1 select_reduce_fusion
  2.4 0.7 copy.55
  3.2 19.8 %all-to-all-start = ((s32[128,1,1]{2,1,0:T(1,128)}), s32[128,1,1]{2,1,0:T(1,128)S(1)}, u32[]{:S(2)}, u32[]{:S(2)}) async-start(s32[128,1,1]{2,1,0:T(1,128)} %copy.55), calls=%async_computation | async-start | bytes 131072 | tf_op jit(solution)/shard_map/all_to_all | solution.py:95
  22.9 1.1 pad_maximum_fusion.3
  24.0 14.4 %all-to-all-done = s32[128,1,1]{2,1,0:T(1,128)S(1)} async-done(((s32[128,1,1]{2,1,0:T(1,128)}), s32[128,1,1]{2,1,0:T(1,128)S(1)}, u32[]{:S(2)}, u32[]{:S(2)}) %all-to-all-start) | async-done | bytes 544 | tf_op jit(solution)/shard_map/all_to_all | solution.py:95
  38.4 2.4 maximum_reduce_fusion
  40.8 6.3 gather_fusion
  47.1 2.4 compare_reduce_fusion
  49.4 7.4 bitcast_select_fusion
  56.9 7.6 all-to-all-start.1
  64.6 1.9 collective-permute-start
  66.5 7.0 collective-permute-start.1
  73.5 0.1 reshape.189
  73.5 0.1 lt.113
  73.7 0.1 copy.52
  73.8 0.3 copy.49
  74.0 0.3 copy.50
  74.3 0.1 copy.51
  74.4 1.8 convolution_bitcast_fusion
  76.2 844.4 %all-reduce.2 = bf16[2,4,2,64,256]{4,2,3,0,1:T(2,128)(2,1)S(1)} all-reduce(f32[2,4,2,64,256]{4,2,3,0,1:T(2,128)} %convolution_bitcast_fusion), channel_id=1, replica_groups=mesh['ctx'=128,'head'=4] {'ctx'}, use_global_device_ids=true, to_apply=%region_0.1 | all-reduce | flops 262144 | bytes 1572864 | tf_op jit(solution)/shard_map/psum | solution.py:80
  920.6 0.1 reduce_sum.32
  920.7 0.1 copy.53
  920.8 0.8 reshape.190
  921.5 0.1 concatenate.13.clone
  921.6 0.1 broadcast_in_dim.78
  921.7 0.1 broadcast_in_dim.79
  921.8 0.1 compare_and_fusion
  921.9 0.0 collective-permute-done
  921.9 0.0 collective-permute-done.1
  921.9 1.1 pad_maximum_fusion
  923.0 0.8 fusion.32
  923.9 0.8 fusion.31
  924.7 0.8 fusion.30
  925.5 1.1 broadcast_dynamic-update-slice_fusion
  926.6 0.0 all-to-all-done.1
  926.6 4.1 gather_fusion.1
  930.7 2.3 bitcast_dynamic-update-slice_fusion
  933.0 5.2 fusion.64
  938.3 4.6 squeeze.7
  942.9 5.7 squeeze.6
  948.6 1.9 fusion.6
  950.5 1.2 fusion.65
  951.7 0.5 copy-done.3
  952.2 0.6 fusion.25
  952.8 0.3 copy.65
  953.0 0.2 reshape.191
  953.2 3.2 collective-permute-start.3
  956.4 2.7 collective-permute-start.2
  959.1 0.3 fusion.38
  959.4 3.9 collective-permute-done.3
  963.3 3.2 collective-permute-start.4
  966.5 0.3 convolution_add_fusion.2
  966.8 0.3 convolution_add_fusion.1
  967.1 4.4 collective-permute-done.4
  971.6 1.1 fusion.14
  (23 shorter events, 0.1 us)
Async XLA Ops:
  0.0 959.1 %copy-start = (bf16[1024,512]{1,0:T(8,128)(2,1)S(1)}, bf16[1024,512]{1,0:T(8,128)(2,1)}, u32[]{:S(2)}) copy-start(bf16[1024,512]{1,0:T(8,128)(2,1)} %param.10) | copy-start | bytes 3145732
  3.2 35.3 %all-to-all-start = ((s32[128,1,1]{2,1,0:T(1,128)}), s32[128,1,1]{2,1,0:T(1,128)S(1)}, u32[]{:S(2)}, u32[]{:S(2)}) async-start(s32[128,1,1]{2,1,0:T(1,128)} %copy.55), calls=%async_computation | async-start | bytes 131072 | tf_op jit(solution)/shard_map/all_to_all | solution.py:95
  56.9 7.6 copy-start.1
  56.9 7.6 copy-start.2
  56.9 16.8 %copy-start.5 = (s32[4,2]{0,1:T(2,128)S(1)}, s32[4,2]{0,1:T(2,128)}, u32[]{:S(2)}) copy-start(s32[4,2]{0,1:T(2,128)} %param.11) | copy-start | bytes 100
  56.9 869.8 %all-to-all-start.1 = ((bf16[128,1,2,64,256]{4,3,2,1,0:T(8,128)(2,1)}), bf16[128,1,2,64,256]{4,3,2,1,0:T(8,128)(2,1)}, u32[]{:S(2)}, u32[]{:S(2)}) async-start(bf16[128,1,2,64,256]{4,3,2,1,0:T(8,128)(2,1)} %bitcast_select_fusion), calls=%async_computation.1 | async-start | bytes 16777216 | tf_op jit(solution)/shard_map/all_to_all | solution.py:108
  64.6 857.3 %collective-permute-start = (bf16[2,4,64,256]{3,2,1,0:T(8,128)(2,1)S(1)}, bf16[2,4,64,256]{3,2,1,0:T(8,128)(2,1)}, u32[]{:S(2)}, u32[]{:S(2)}) collective-permute-start(bf16[2,4,64,256]{3,2,1,0:T(8,128)(2,1)S(1)} %get-tuple-element.7), channel_id=1, source_target_pairs={{0,4},{4,8},{8,12},{12,16},{16,20},{20,24},{24,28},{28,32},{32,36}... | collective-permute-start | bytes 786440 | tf_op jit(solution)/shard_map/ppermute | solution.py:35
  66.5 855.4 %collective-permute-start.1 = (bf16[2,4,64,256]{3,2,1,0:T(8,128)(2,1)S(1)}, bf16[2,4,64,256]{3,2,1,0:T(8,128)(2,1)}, u32[]{:S(2)}, u32[]{:S(2)}) collective-permute-start(bf16[2,4,64,256]{3,2,1,0:T(8,128)(2,1)S(1)} %get-tuple-element.8), channel_id=1, source_target_pairs={{4,0},{8,4},{12,8},{16,12},{20,16},{24,20},{28,24},{32,28},{36,32}... | collective-permute-start | bytes 786440 | tf_op jit(solution)/shard_map/ppermute | solution.py:37
  74.4 846.3 %copy-start.4 = (bf16[4,128,256]{2,1,0:T(8,128)(2,1)S(1)}, bf16[4,128,256]{2,1,0:T(8,128)(2,1)}, u32[]{:S(2)}) copy-start(bf16[4,128,256]{2,1,0:T(8,128)(2,1)} %param.7) | copy-start | bytes 786436
  950.5 1.7 copy-start.3
  953.2 10.1 %collective-permute-start.3 = (bf16[4,128,256]{2,1,0:T(8,128)(2,1)S(1)}, bf16[4,128,256]{2,1,0:T(8,128)(2,1)S(1)}, u32[]{:S(2)}, u32[]{:S(2)}) collective-permute-start(bf16[4,128,256]{2,1,0:T(8,128)(2,1)S(1)} %reshape.191), channel_id=1, source_target_pairs={{0,1},{1,2},{2,3},{3,0},{4,5},{5,6},{6,7},{7,4},{8,9},{9,10},{10,1... | collective-permute-start | bytes 786440 | tf_op jit(solution)/shard_map/ppermute | solution.py:20
  956.4 10.1 %collective-permute-start.2 = (bf16[4,128,256]{2,1,0:T(8,128)(2,1)S(1)}, bf16[4,128,256]{2,1,0:T(8,128)(2,1)S(1)}, u32[]{:S(2)}, u32[]{:S(2)}) collective-permute-start(bf16[4,128,256]{2,1,0:T(8,128)(2,1)S(1)} %reshape.191), channel_id=1, source_target_pairs={{0,3},{1,0},{2,1},{3,2},{4,7},{5,4},{6,5},{7,6},{8,11},{9,8},{10,9... | collective-permute-start | bytes 786440 | tf_op jit(solution)/shard_map/ppermute | solution.py:22
  963.3 8.3 collective-permute-start.4
